TPU v7x, 512 devices: a whole 4x8x8 slice. The times are simulated.
512 devices in a mesh: dp: 16 (over z, core), cls: 32 (over x, y).
Axes of the slice: x: 4, y: 8, z: 8, core: 2. Of those that a mesh axis runs over, the one named last changes fastest.
Arguments:
- embeddings: bfloat16 [131072, 768], P(('dp', 'cls'))
- class_rows: bfloat16 [128, 256, 768], P('cls')
- cand_blocks: int32 [1024, 8], P(('dp', 'cls')), may hold values from 0 to 127, all different within a row; in each aligned block of 64 rows (0 to 63, 64 to 127, ...) at most 8 rows name the same one
- label_pos: int32 [131072], P(('dp', 'cls')), may hold values from 0 to 2047
Outputs:
- image_loss: float32 [131072], P('dp')
- class_grad: float32 [256, 128, 768], P('dp', 'cls')
Inputs may be any that keep to these rules, and one draw needn't show every extreme that they name: `cand_blocks`: the 8 blocks of one list differ; block n lives on index n // 4 of cls. Among the 64 lists of one index of dp no block is named by more than 8 lists, and in some index of dp one block is named by exactly 8.
All inputs are finite; a program needn't handle non-finite values.
Results may differ from a plain program's by a relative error of at most 0.00099.
Values may be sent and summed in bfloat16 or wider, within the bound.
A program may use at most 64 MiB of HBM per device.

v0:
```python
import jax
import jax.numpy as jnp
from jax import lax
from jax.sharding import PartitionSpec as P

MOST = 8
NEG = -1e30


def body(embeddings, class_rows, cand_blocks, label_pos):
    gathered, cand_all, labels_all = (
        lax.all_gather(embeddings, "cls", axis=0, tiled=True),
        lax.all_gather(cand_blocks, "cls", axis=0, tiled=True),
        lax.all_gather(label_pos, "cls", axis=0, tiled=True),
    )
    local_blocks, block_taxa, feature_width = class_rows.shape
    group_lists = cand_all.shape[0]
    dp_images = gathered.shape[0]
    group_rows = dp_images // group_lists
    my_shard = lax.axis_index("cls")
    owned_ids = my_shard * local_blocks + jnp.arange(local_blocks, dtype=jnp.int32)
    matches = (cand_all[:, :, None] == owned_ids[None, None, :]).astype(jnp.int32)
    hit_count = jnp.sum(matches, axis=1)
    slot_of = jnp.sum(
        matches * jnp.arange(cand_all.shape[1], dtype=jnp.int32)[None, :, None], axis=1
    )
    hit_rank = jnp.cumsum(hit_count, axis=0) - 1
    slot_ids = jnp.arange(MOST, dtype=jnp.int32)
    picked = (
        (hit_count[:, :, None] > 0) & (hit_rank[:, :, None] == slot_ids[None, None, :])
    ).astype(jnp.int32)
    block_index = jnp.arange(group_lists, dtype=jnp.int32)[:, None, None]
    src_block = jnp.sum(picked * block_index, axis=0)
    valid_slot = jnp.sum(picked, axis=0)
    src_slot = jnp.sum(picked * slot_of[:, :, None], axis=0)
    image_tiles = gathered.reshape(group_lists, group_rows, feature_width)[src_block]
    label_tiles = labels_all.reshape(group_lists, group_rows)[src_block]
    scores = jnp.einsum(
        "jsid,jtd->jsit", image_tiles, class_rows, preferred_element_type=jnp.float32
    )
    live_slot = (valid_slot > 0)[:, :, None, None]
    target_pos = (
        src_slot[:, :, None, None] * block_taxa
        + jnp.arange(block_taxa, dtype=jnp.int32)[None, None, None, :]
    )
    is_true = (label_tiles[:, :, :, None] == target_pos) & live_slot
    true_slot = jnp.sum(jnp.where(is_true, scores, 0.0), axis=3)
    slot_max = jnp.max(scores, axis=3)
    owner_map = picked.reshape(group_lists, local_blocks * MOST)
    owner_float = owner_map.astype(jnp.float32)
    flat_max = slot_max.reshape(local_blocks * MOST, group_rows)
    local_max = jnp.max(jnp.where(owner_map[:, :, None] > 0, flat_max[None, :, :], NEG), axis=1)
    local_true = jnp.einsum(
        "bq,qi->bi", owner_float, true_slot.reshape(-1, group_rows), precision=lax.Precision.HIGHEST
    )
    score_max = lax.pmax(local_max.astype(jnp.bfloat16), "cls").astype(local_max.dtype)
    per_slot = score_max[src_block]
    exp_weights = jnp.where(live_slot, jnp.exp(scores - per_slot[:, :, :, None]), 0.0)
    exp_total, true_total = lax.psum(
        (
            jnp.einsum(
                "bq,qi->bi",
                owner_float,
                jnp.sum(exp_weights, axis=3).reshape(-1, group_rows),
                precision=lax.Precision.HIGHEST,
            ),
            local_true,
        ),
        "cls",
    )
    log_norm = score_max + jnp.log(exp_total)
    image_loss = (log_norm - true_total).reshape(dp_images)
    softmax_prob = jnp.exp(scores - log_norm[src_block][:, :, :, None])
    logit_grad = jnp.where(live_slot, softmax_prob - is_true.astype(jnp.float32), 0.0).astype(
        jnp.bfloat16
    )
    row_share = block_taxa // lax.axis_size("dp")
    whole_sum = lax.psum(
        jnp.einsum("jsit,jsid->tjd", logit_grad, image_tiles, preferred_element_type=jnp.float32),
        "dp",
    )
    class_grad = lax.dynamic_slice_in_dim(whole_sum, lax.axis_index("dp") * row_share, row_share, 0)
    return (image_loss, class_grad)


def solution(mesh):
    in_specs = (
        P(("dp", "cls"), None),
        P("cls", None, None),
        P(("dp", "cls"), None),
        P(("dp", "cls")),
    )
    out_specs = (P("dp"), P("dp", "cls", None))
    return jax.shard_map(body, mesh=mesh, in_specs=in_specs, out_specs=out_specs, check_vma=False)
```

profile of v0, /device:TPU:1, one launch (start us, length us, event | category | flops | bytes accessed | tf_op | source)
XLA Modules:
  0.0 591.8 jit_solution(9255299646218935432)
XLA Ops:
  7.2 0.7 all-gather.4.cloned.1.call-update
  8.0 33.4 %all-gather = s32[32,2,8]{2,1,0:T(2,128)S(1)} all-gather(s32[1,2,8]{2,1,0:T(2,128)} %bitcast.56), channel_id=1, replica_groups=mesh['dp'=16,'cls'=32] {'cls'}, dimensions={0}, use_global_device_ids=true | all-gather | bytes 2112 | tf_op jit(solution)/shard_map/all_gather | solution.py:13
  41.4 0.1 fusion.10
  41.5 0.1 copy.27
  41.8 0.3 select_reduce_fusion.3
  42.4 0.1 copy.29
  42.5 30.6 %all-gather.1 = s32[32,1,256]{2,1,0:T(1,128)S(1)} all-gather(s32[1,1,256]{2,1,0:T(1,128)} %bitcast.57), channel_id=1, replica_groups=mesh['dp'=16,'cls'=32] {'cls'}, dimensions={0}, use_global_device_ids=true | all-gather | bytes 33792 | tf_op jit(solution)/shard_map/all_gather | solution.py:14
  73.1 0.6 gather_fusion.2
  73.8 66.1 %all-gather.4.cloned.1.call-done = bf16[8192,768]{1,0:T(8,128)(2,1)} async-done(((bf16[256,768]{1,0:T(8,128)(2,1)}), bf16[8192,768]{1,0:T(8,128)(2,1)}) %all-gather.4.cloned.1.call-update) | async-done | bytes 12582928 | tf_op jit(solution)/shard_map/all_gather | solution.py:12
  139.9 8.1 %gather_fusion = bf16[32,128,768]{2,1,0:T(8,128)(2,1)} fusion(bf16[64,128,768]{2,1,0:T(8,128)(2,1)} %bitcast.48, s32[1024]{0:T(1024)S(1)} %pad_clamp_fusion), kind=kCustom, calls=%fused_computation | custom fusion | bytes 12583040 | tf_op jit(solution)/shard_map/gather | solution.py:36
  148.1 6.5 %fusion.20 = (bf16[4,8,128]{2,1,0:T(8,128)(2,1)S(1)}, f32[4,8,128,256]{3,2,1,0:T(8,128)}) fusion(bf16[4,8,128,768]{3,2,1,0:T(8,128)(2,1)} %bitcast.46, bf16[4,256,768]{2,1,0:T(8,128)(2,1)S(1)} %copy-done), kind=kOutput, calls=%fused_computation.49 | convolution fusion | flops 1611657216 | bytes 12066816 | tf_op jit(solution)/shard_map/jsid,jtd->jsit/dot_general | solution.py:38
  154.6 0.4 select_reduce_fusion.2
  155.0 111.6 %pmax.7 = bf16[64,128]{1,0:T(8,128)(2,1)S(1)} all-reduce(bf16[64,128]{1,0:T(8,128)(2,1)S(1)} %select_reduce_fusion.2), channel_id=1, replica_groups=mesh['dp'=16,'cls'=32] {'cls'}, use_global_device_ids=true, to_apply=%region_5.6 | all-reduce | flops 8192 | bytes 32768 | tf_op jit(solution)/shard_map/pmax | solution.py:56
  266.6 0.6 gather_fusion.1
  267.2 5.0 select_reduce_fusion
  272.2 0.9 convolution_bitcast_fusion
  273.0 0.9 convolution_bitcast_fusion.1
  273.9 170.9 %all-reduce.6.cloned.1.call-done = (f32[64,128]{1,0:T(8,128)}, f32[64,128]{1,0:T(8,128)}) async-done(((f32[64,128]{1,0:T(8,128)}, f32[64,128]{1,0:T(8,128)}), (f32[64,128]{1,0:T(8,128)}, f32[64,128]{1,0:T(8,128)})) %all-reduce.6.cloned.1.call-update) | async-done | bytes 65552 | tf_op jit(solution)/shard_map/psum | solution.py:59
  444.9 1.4 subtract_bitcast_fusion
  446.3 0.6 gather_fusion.3
  446.9 7.6 %fusion.6 = f32[256,4,768]{0,2,1:T(8,128)} fusion(bf16[4,8,128,768]{3,2,1,0:T(8,128)(2,1)} %bitcast.47, f32[4,8,128,256]{3,2,1,0:T(8,128)} %get-tuple-element.22, f32[4,8,128]{2,1,0:T(8,128)S(1)} %bitcast.54, s32[4,8,256]{2,1,0:T(8,128)S(1)} %iota_add_fusion, s32[4,8,128]{2,1,0:T(8,128)S(1)} %bitcast.52, pred[4,8]{1,0:T(4,128)(4,1)S(1)} %broadcast_compare_fusion), kind=kOutput, calls=%fused_computation.14 | convolution fusion | flops 1617952768 | bytes 13697056 | tf_op jit(solution)/shard_map/jsit,jsid->tjd/dot_general | solution.py:79
  454.5 127.7 %all-reduce.4.cloned.1.call-done = f32[256,4,768]{0,2,1:T(8,128)} async-done(((f32[256,4,768]{0,2,1:T(8,128)}), f32[256,4,768]{0,2,1:T(8,128)}) %all-reduce.4.cloned.1.call-update) | async-done | bytes 3145744 | tf_op jit(solution)/shard_map/psum | solution.py:78
  582.2 1.9 constant_dynamic-slice_fusion
  584.1 1.1 copy.32
  (23 shorter events, 0.7 us)
Async XLA Ops:
  7.2 140.9 %copy-start = (bf16[4,256,768]{2,1,0:T(8,128)(2,1)S(1)}, bf16[4,256,768]{2,1,0:T(8,128)(2,1)}, u32[]{:S(2)}) copy-start(bf16[4,256,768]{2,1,0:T(8,128)(2,1)} %param.5) | copy-start | bytes 4718596
  7.2 132.8 %all-gather.4.cloned.1.call-start = ((), (), s32[]{:S(2)}) async-start(), calls=%async_computation | async-start | bytes 12976128 | tf_op jit(solution)/shard_map/all_gather | solution.py:12
  7.9 437.0 %all-reduce.6.cloned.1.call-start = ((), (), s32[]{:S(2)}) async-start(), calls=%async_computation.2 | async-start | bytes 131072 | tf_op jit(solution)/shard_map/psum | solution.py:59
  273.9 308.3 %all-reduce.4.cloned.1.call-start = ((), (), s32[]{:S(2)}) async-start(), calls=%async_computation.1 | async-start | bytes 6291456 | tf_op jit(solution)/shard_map/psum | solution.py:78
Sparse Core Ops, SparseCore 0:
  11.1 128.7 all-gather.3
  274.0 170.8 all-reduce.5
  454.6 127.5 all-reduce.3
where the time goes:
time: 592 us
  waiting for transfers between devices  366 us (62%)
  blocking collectives  176 us (30%)
  matrix products  15.9 us (3%)
  between operations  13.8 us (2%)
  local copies, waits for them, and re-layouts  13.4 us (2%)
  other arithmetic  7.47 us (1%)
    psum x1, waiting for transfers between devices, body(): lax.psum((jnp.einsum('bq,qi->bi', owner_float, jnp.sum(exp_weights, axis=...  171 us
    psum x1, waiting for transfers between devices, body(): lax.psum(jnp.einsum('jsit,jsid->tjd', logit_grad, image_tiles, preferred_...  128 us
    pmax x1, blocking collectives, body(): lax.pmax(local_max.astype(jnp.bfloat16), 'cls').astype(local_max.dtype)  112 us
    all_gather x1, waiting for transfers between devices, body(): lax.all_gather(embeddings, 'cls', axis=0, tiled=True)  66.1 us
    all_gather x1, blocking collectives, body(): lax.all_gather(cand_blocks, 'cls', axis=0, tiled=True)  33.4 us
    all_gather x1, blocking collectives, body(): lax.all_gather(label_pos, 'cls', axis=0, tiled=True)  30.6 us
  transfers between devices with their start and end apart: 3, of which 3 were waited for; matrix products, arithmetic and copies ran while one was open for 0% of the time, Pallas kernels for 0%

commit v1 on v0

--- a/solution.py
+++ b/solution.py
@@ -5,12 +5,15 @@
 
 MOST = 8
 NEG = -1e30
+plan_ticks = lambda ax_name, packet: jnp.concatenate(
+    lax.all_to_all(jnp.stack(lax.axis_size(ax_name) * [packet]), ax_name, 0, 0), axis=0
+)
 
 
 def body(embeddings, class_rows, cand_blocks, label_pos):
     gathered, cand_all, labels_all = (
         lax.all_gather(embeddings, "cls", axis=0, tiled=True),
-        lax.all_gather(cand_blocks, "cls", axis=0, tiled=True),
+        plan_ticks("cls", cand_blocks),
         lax.all_gather(label_pos, "cls", axis=0, tiled=True),
     )
     local_blocks, block_taxa, feature_width = class_rows.shape

time: 592 us -> 592 us (level)
  blocking collectives: 176 us -> 145 us
  waiting for transfers between devices: 366 us -> 384 us
  starting transfers between devices: 0.12 us -> 10.6 us
    all_gather x1 -> x0, blocking collectives: 33.4 us -> none  [body(): lax.all_gather(cand_blocks, 'cls', axis=0, tiled=True)]
    all_gather x1, waiting for transfers between devices: 66.1 us -> 84.8 us  [body(): lax.all_gather(embeddings, 'cls', axis=0, tiled=True)]
    all_to_all x0 -> x1, starting transfers between devices: none -> 10.5 us  [lax.all_to_all(jnp.stack(lax.axis_size(ax_name) * [packet]), ax_name, 0, 0)]
  transfers between devices with their start and end apart: 3 -> 4, of which waited for: 3 -> 3; matrix products, arithmetic and copies ran while one was open for 0% -> 1% of each run, Pallas kernels for 0% -> 0%
where the time goes in v1:
time: 592 us
  waiting for transfers between devices  384 us (65%)
  blocking collectives  145 us (24%)
  matrix products  15.9 us (3%)
  local copies, waits for them, and re-layouts  14.7 us (2%)
  between operations  13.8 us (2%)
  starting transfers between devices  10.6 us (2%)
  other arithmetic  7.47 us (1%)
    psum x1, waiting for transfers between devices, body(): lax.psum((jnp.einsum('bq,qi->bi', owner_float, jnp.sum(exp_weights, axis=...  171 us
    psum x1, waiting for transfers between devices, body(): lax.psum(jnp.einsum('jsit,jsid->tjd', logit_grad, image_tiles, preferred_...  128 us
    pmax x1, blocking collectives, body(): lax.pmax(local_max.astype(jnp.bfloat16), 'cls').astype(local_max.dtype)  112 us
    all_gather x1, waiting for transfers between devices, body(): lax.all_gather(embeddings, 'cls', axis=0, tiled=True)  84.8 us
    all_gather x1, blocking collectives, body(): lax.all_gather(label_pos, 'cls', axis=0, tiled=True)  33.3 us
  transfers between devices with their start and end apart: 4, of which 3 were waited for; matrix products, arithmetic and copies ran while one was open for 1% of the time, Pallas kernels for 0%

profile of v1, /device:TPU:1, one launch (start us, length us, event | category | flops | bytes accessed | tf_op | source)
XLA Modules:
  0.0 591.5 jit_solution(16067459114633269120)
XLA Ops:
  7.2 0.7 all-gather.3.cloned.1.call-update
  7.9 1.3 stack.2
  9.2 10.5 %all-to-all-start = ((s32[32,2,8]{2,1,0:T(2,128)}), s32[32,2,8]{2,1,0:T(2,128)S(1)}, u32[]{:S(2)}, u32[]{:S(2)}) async-start(s32[32,2,8]{2,1,0:T(2,128)} %stack.2), calls=%async_computation | async-start | bytes 65536 | tf_op jit(solution)/shard_map/all_to_all | solution.py:9
  19.8 33.3 %all-gather = s32[32,1,256]{2,1,0:T(1,128)S(1)} all-gather(s32[1,1,256]{2,1,0:T(1,128)} %bitcast.55), channel_id=1, replica_groups=mesh['dp'=16,'cls'=32] {'cls'}, dimensions={0}, use_global_device_ids=true | all-gather | bytes 33792 | tf_op jit(solution)/shard_map/all_gather | solution.py:17
  53.3 0.1 fusion.10
  53.6 0.3 select_reduce_fusion.3
  54.1 0.1 copy.37
  54.2 0.6 gather_fusion.2
  54.9 84.8 %all-gather.3.cloned.1.call-done = bf16[8192,768]{1,0:T(8,128)(2,1)} async-done(((bf16[256,768]{1,0:T(8,128)(2,1)}), bf16[8192,768]{1,0:T(8,128)(2,1)}) %all-gather.3.cloned.1.call-update) | async-done | bytes 12582928 | tf_op jit(solution)/shard_map/all_gather | solution.py:15
  139.7 8.1 %gather_fusion = bf16[32,128,768]{2,1,0:T(8,128)(2,1)} fusion(bf16[64,128,768]{2,1,0:T(8,128)(2,1)} %bitcast.47, s32[1024]{0:T(1024)S(1)} %pad_clamp_fusion), kind=kCustom, calls=%fused_computation | custom fusion | bytes 12583040 | tf_op jit(solution)/shard_map/gather | solution.py:39
  147.9 6.5 %fusion.20 = (bf16[4,8,128]{2,1,0:T(8,128)(2,1)S(1)}, f32[4,8,128,256]{3,2,1,0:T(8,128)}) fusion(bf16[4,8,128,768]{3,2,1,0:T(8,128)(2,1)} %bitcast.45, bf16[4,256,768]{2,1,0:T(8,128)(2,1)S(1)} %copy-done), kind=kOutput, calls=%fused_computation.49 | convolution fusion | flops 1611657216 | bytes 12066816 | tf_op jit(solution)/shard_map/jsid,jtd->jsit/dot_general | solution.py:41
  154.4 0.4 select_reduce_fusion.2
  154.8 111.6 %pmax.7 = bf16[64,128]{1,0:T(8,128)(2,1)S(1)} all-reduce(bf16[64,128]{1,0:T(8,128)(2,1)S(1)} %select_reduce_fusion.2), channel_id=1, replica_groups=mesh['dp'=16,'cls'=32] {'cls'}, use_global_device_ids=true, to_apply=%region_5.6 | all-reduce | flops 8192 | bytes 32768 | tf_op jit(solution)/shard_map/pmax | solution.py:59
  266.4 0.6 gather_fusion.1
  267.0 5.0 select_reduce_fusion
  272.0 0.9 convolution_bitcast_fusion
  272.8 0.9 convolution_bitcast_fusion.1
  273.7 170.9 %all-reduce.6.cloned.1.call-done = (f32[64,128]{1,0:T(8,128)}, f32[64,128]{1,0:T(8,128)}) async-done(((f32[64,128]{1,0:T(8,128)}, f32[64,128]{1,0:T(8,128)}), (f32[64,128]{1,0:T(8,128)}, f32[64,128]{1,0:T(8,128)})) %all-reduce.6.cloned.1.call-update) | async-done | bytes 65552 | tf_op jit(solution)/shard_map/psum | solution.py:62
  444.6 1.4 subtract_bitcast_fusion
  446.0 0.6 gather_fusion.3
  446.6 7.6 %fusion.6 = f32[256,4,768]{0,2,1:T(8,128)} fusion(bf16[4,8,128,768]{3,2,1,0:T(8,128)(2,1)} %bitcast.46, f32[4,8,128,256]{3,2,1,0:T(8,128)} %get-tuple-element.24, f32[4,8,128]{2,1,0:T(8,128)S(1)} %bitcast.53, s32[4,8,256]{2,1,0:T(8,128)S(1)} %iota_add_fusion, s32[4,8,128]{2,1,0:T(8,128)S(1)} %bitcast.51, pred[4,8]{1,0:T(4,128)(4,1)S(1)} %broadcast_compare_fusion), kind=kOutput, calls=%fused_computation.14 | convolution fusion | flops 1617952768 | bytes 13697056 | tf_op jit(solution)/shard_map/jsit,jsid->tjd/dot_general | solution.py:82
  454.3 127.7 %all-reduce.4.cloned.1.call-done = f32[256,4,768]{0,2,1:T(8,128)} async-done(((f32[256,4,768]{0,2,1:T(8,128)}), f32[256,4,768]{0,2,1:T(8,128)}) %all-reduce.4.cloned.1.call-update) | async-done | bytes 3145744 | tf_op jit(solution)/shard_map/psum | solution.py:81
  582.0 1.9 constant_dynamic-slice_fusion
  583.9 1.1 copy.40
  (25 shorter events, 0.8 us)
Async XLA Ops:
  7.2 140.7 %copy-start = (bf16[4,256,768]{2,1,0:T(8,128)(2,1)S(1)}, bf16[4,256,768]{2,1,0:T(8,128)(2,1)}, u32[]{:S(2)}) copy-start(bf16[4,256,768]{2,1,0:T(8,128)(2,1)} %param.5) | copy-start | bytes 4718596
  7.2 132.6 %all-gather.3.cloned.1.call-start = ((), (), s32[]{:S(2)}) async-start(), calls=%async_computation.1 | async-start | bytes 12976128 | tf_op jit(solution)/shard_map/all_gather | solution.py:15
  9.2 44.0 %all-to-all-start = ((s32[32,2,8]{2,1,0:T(2,128)}), s32[32,2,8]{2,1,0:T(2,128)S(1)}, u32[]{:S(2)}, u32[]{:S(2)}) async-start(s32[32,2,8]{2,1,0:T(2,128)} %stack.2), calls=%async_computation | async-start | bytes 65536 | tf_op jit(solution)/shard_map/all_to_all | solution.py:9
  19.7 424.9 %all-reduce.6.cloned.1.call-start = ((), (), s32[]{:S(2)}) async-start(), calls=%async_computation.3 | async-start | bytes 131072 | tf_op jit(solution)/shard_map/psum | solution.py:62
  273.7 308.3 %all-reduce.4.cloned.1.call-start = ((), (), s32[]{:S(2)}) async-start(), calls=%async_computation.2 | async-start | bytes 6291456 | tf_op jit(solution)/shard_map/psum | solution.py:81
Sparse Core Ops, SparseCore 0:
  11.1 128.5 all-gather.2
  273.8 170.7 all-reduce.5
  454.4 127.5 all-reduce.3
